TPU v7x, 32 devices: a whole 2x2x4 slice. The times are simulated.
32 devices in a mesh: dap: 8 (over z, core), ch: 4 (over y, x).
Axes of the slice: x: 2, y: 2, z: 4, core: 2. Of those that a mesh axis runs over, the one named last changes fastest.
Arguments:
- pair_rep: bfloat16 [120, 120, 128], P('dap', 'ch'), may hold values from -400 to 400
- residue_mask: int32 [120], replicated, may hold values 0 or 1
- w_proj: bfloat16 [128, 512], replicated, may hold values from -0.5 to 0.5
- w_gate: bfloat16 [128, 128], replicated, may hold values from -0.5 to 0.5
- w_out: bfloat16 [128, 128], replicated, may hold values from -0.5 to 0.5
- cotangent: bfloat16 [120, 120, 128], P('dap', 'ch'), may hold values from -6 to 6
Outputs:
- pair_update: bfloat16 [120, 120, 128], P('dap', 'ch')
- grad_pair: bfloat16 [120, 120, 128], P('dap', 'ch')
Inputs may be any that keep to these rules, and one draw needn't show every extreme that they name: `residue_mask`: 1 marks a residue of the crop, 0 a padding position.
All inputs are finite; a program needn't handle non-finite values.
Results may differ from a plain program's by a relative error of at most 0.0085.
Values may be sent and summed in bfloat16 or wider, within the bound.
No kernel may reach another device: no remote copies, remote signals or barrier semaphores. Data moves between devices by JAX's collectives and lax.ppermute only.
A program may use at most 64 MiB of HBM per device.

v0:
```python
import jax
import jax.numpy as jnp
from jax import lax
from jax.sharding import PartitionSpec as P

EPSILON = 1e-05


def normalize(values, axis):
    center = jnp.mean(values, axis=axis, keepdims=True)
    spread = values - center
    scale_inv = lax.rsqrt(jnp.mean(spread * spread, axis=axis, keepdims=True) + EPSILON)
    return (spread * scale_inv, scale_inv)


def norm_back(grad_in, normed, scale_inv, axis):
    first = jnp.mean(grad_in, axis=axis, keepdims=True)
    second = jnp.mean(grad_in * normed, axis=axis, keepdims=True)
    return scale_inv * (grad_in - first - normed * second)


def on_device(pair_rep, residue_mask, w_proj, w_gate, w_out, cotangent):
    row_count, columns, channels = pair_rep.shape
    hidden_width = w_out.shape[0]
    row_start = lax.axis_index("dap") * row_count
    col_start = lax.axis_index("ch") * columns
    live_flags = residue_mask.astype(jnp.float32)
    row_live = lax.dynamic_slice_in_dim(live_flags, row_start, row_count, 0)
    col_live = lax.dynamic_slice_in_dim(live_flags, col_start, columns, 0)
    cell_mask = row_live[:, None] * col_live[None, :]
    normed, pair_scale = normalize(pair_rep.astype(jnp.float32), 2)
    normed_half = normed.astype(jnp.bfloat16)
    projected = jnp.einsum("rkd,de->erk", normed_half, w_proj, preferred_element_type=jnp.float32)
    left_sig = jax.nn.sigmoid(projected[:hidden_width])
    left_val = projected[hidden_width : 2 * hidden_width]
    right_sig = jax.nn.sigmoid(projected[2 * hidden_width : 3 * hidden_width])
    right_val = projected[3 * hidden_width :]
    left_cells = (left_sig * left_val * cell_mask).astype(jnp.bfloat16)
    right_cells = (right_sig * right_val * cell_mask).astype(jnp.bfloat16)
    gate_values = jax.nn.sigmoid(
        jnp.einsum("rkd,de->rke", normed_half, w_gate, preferred_element_type=jnp.float32)
    )
    left_rows, right_rows = (
        lax.all_to_all(left_cells, "ch", split_axis=0, concat_axis=2, tiled=True),
        lax.all_to_all(right_cells, "ch", split_axis=0, concat_axis=2, tiled=True),
    )
    product = jnp.einsum(
        "cik,cjk->cij",
        left_rows,
        lax.all_gather(right_rows, "dap", axis=1, tiled=True),
        preferred_element_type=jnp.float32,
    ).astype(jnp.bfloat16)
    product_cells = lax.all_to_all(product, "ch", split_axis=2, concat_axis=0, tiled=True)
    hidden_norm, hidden_scale = normalize(product_cells.astype(jnp.float32), 0)
    hidden_half = hidden_norm.astype(jnp.bfloat16)
    projected_out = jnp.einsum(
        "hrk,hd->rkd", hidden_half, w_out, preferred_element_type=jnp.float32
    )
    pair_update = (gate_values * projected_out).astype(jnp.bfloat16)
    upstream = cotangent.astype(jnp.float32)
    grad_out = (upstream * gate_values).astype(jnp.bfloat16)
    grad_logit = (upstream * projected_out * gate_values * (1.0 - gate_values)).astype(jnp.bfloat16)
    grad_hidden = jnp.einsum("rkd,hd->hrk", grad_out, w_out, preferred_element_type=jnp.float32)
    grad_product = norm_back(grad_hidden, hidden_norm, hidden_scale, 0).astype(jnp.bfloat16)
    grad_rows = lax.all_to_all(grad_product, "ch", split_axis=0, concat_axis=2, tiled=True)
    piece_left = lax.all_gather(left_rows, "dap", axis=1, tiled=True)
    piece_right = lax.all_gather(right_rows, "dap", axis=1, tiled=True)
    piece_grad = lax.all_gather(grad_rows, "dap", axis=1, tiled=True)
    cross_slab = lax.dynamic_slice_in_dim(piece_grad, row_start, row_count, 2)
    new_left = jnp.einsum(
        "cij,cjk->cik", grad_rows, piece_right, preferred_element_type=jnp.float32
    )
    new_right = jnp.einsum(
        "cij,cik->cjk", cross_slab, piece_left, preferred_element_type=jnp.float32
    )
    left_back, right_back = (
        lax.all_to_all(
            new_left.astype(jnp.bfloat16), "ch", split_axis=2, concat_axis=0, tiled=True
        ),
        lax.all_to_all(
            new_right.astype(jnp.bfloat16), "ch", split_axis=2, concat_axis=0, tiled=True
        ),
    )
    masked_left = left_back.astype(jnp.float32) * cell_mask
    masked_right = right_back.astype(jnp.float32) * cell_mask
    grad_proj = jnp.concatenate(
        [
            masked_left * left_val * left_sig * (1.0 - left_sig),
            masked_left * left_sig,
            masked_right * right_val * right_sig * (1.0 - right_sig),
            masked_right * right_sig,
        ],
        axis=0,
    ).astype(jnp.bfloat16)
    grad_normed = jnp.einsum("erk,de->rkd", grad_proj, w_proj, preferred_element_type=jnp.float32)
    grad_normed = grad_normed + jnp.einsum(
        "rke,de->rkd", grad_logit, w_gate, preferred_element_type=jnp.float32
    )
    grad_pair = norm_back(grad_normed, normed, pair_scale, 2).astype(jnp.bfloat16)
    return (pair_update, grad_pair)


def solution(mesh):
    return jax.shard_map(
        on_device,
        mesh=mesh,
        in_specs=(P("dap", "ch", None), P(), P(), P(), P(), P("dap", "ch", None)),
        out_specs=(P("dap", "ch", None), P("dap", "ch", None)),
        check_vma=False,
    )
```

profile of v0, /device:TPU:0, one launch (start us, length us, event | category | flops | bytes accessed | tf_op | source)
XLA Modules:
  0.0 124.0 jit_solution(5858120735575920195)
XLA Ops:
  0.7 1.1 convert_reduce_fusion
  3.9 1.3 %reshape.95 = bf16[4,2,7200]{2,1,0:T(2,128)(2,1)} reshape(bf16[128,15,30]{2,1,0:T(8,128)(2,1)S(1)} %copy.73) | data formatting | bytes 230400
  5.2 5.2 %all-to-all-start.1 = ((bf16[4,2,7200]{2,1,0:T(2,128)(2,1)}), bf16[4,2,7200]{2,1,0:T(2,128)(2,1)S(1)}, u32[]{:S(2)}, u32[]{:S(2)}) async-start(bf16[4,2,7200]{2,1,0:T(2,128)(2,1)} %reshape.95), calls=%async_computation.1 | async-start | bytes 233472 | tf_op jit(solution)/shard_map/all_to_all | solution.py:45
  10.9 1.3 %reshape.97 = bf16[4,2,7200]{2,1,0:T(2,128)(2,1)} reshape(bf16[128,15,30]{2,1,0:T(8,128)(2,1)S(1)} %copy.71) | data formatting | bytes 230400
  12.2 3.2 %all-to-all-done.1 = bf16[4,2,7200]{2,1,0:T(2,128)(2,1)S(1)} async-done(((bf16[4,2,7200]{2,1,0:T(2,128)(2,1)}), bf16[4,2,7200]{2,1,0:T(2,128)(2,1)S(1)}, u32[]{:S(2)}, u32[]{:S(2)}) %all-to-all-start.1) | async-done | bytes 115232 | tf_op jit(solution)/shard_map/all_to_all | solution.py:45
  15.4 3.3 %all-to-all-start = ((bf16[4,2,7200]{2,1,0:T(2,128)(2,1)}), bf16[4,2,7200]{2,1,0:T(2,128)(2,1)S(1)}, u32[]{:S(2)}, u32[]{:S(2)}) async-start(bf16[4,2,7200]{2,1,0:T(2,128)(2,1)} %reshape.97), calls=%async_computation | async-start | bytes 233472 | tf_op jit(solution)/shard_map/all_to_all | solution.py:44
  20.0 17.0 %all_gather.10 = bf16[32,120,120]{2,0,1:T(8,128)(2,1)S(1)} all-gather(bf16[32,15,120]{2,0,1:T(8,128)(2,1)S(1)} %all_to_all.67), channel_id=1, replica_groups=mesh['dap'=8,'ch'=4] {'dap'}, dimensions={1}, use_global_device_ids=true | all-gather | bytes 1036800 | tf_op jit(solution)/shard_map/all_gather | solution.py:50
  39.7 8.9 %all_to_all.81 = bf16[4,2,7200]{2,1,0:T(2,128)(2,1)S(1)} all-to-all(bf16[4,2,7200]{2,1,0:T(2,128)(2,1)S(1)} %reshape.99), channel_id=1, replica_groups=mesh['dap'=8,'ch'=4] {'ch'}, dimensions={0} | all-to-all | bytes 230400 | tf_op jit(solution)/shard_map/all_to_all | solution.py:53
  49.2 1.0 copy.78
  50.2 1.3 %reshape.89 = f32[32,15,4,30]{3,2,0,1:T(4,128)S(1)} reshape(bf16[32,15,120]{2,0,1:T(8,128)(2,1)} %copy.78) | data formatting | bytes 345600 | tf_op jit(solution)/shard_map/convert_element_type | solution.py:54
  51.7 1.7 %copy.79 = f32[4,32,15,30]{1,0,3,2:T(4,128)} copy(f32[4,32,15,30]{3,0,1,2:T(4,128)S(1)} %bitcast.66) | data formatting | bytes 460800 | tf_op jit(solution)/shard_map/convert_element_type | solution.py:54
  53.5 1.6 %reshape.85 = f32[128,15,30]{0,2,1:T(8,128)S(1)} reshape(f32[4,32,15,30]{1,0,3,2:T(4,128)} %copy.79) | data formatting | bytes 460800 | tf_op jit(solution)/shard_map/convert_element_type | solution.py:54
  59.1 1.3 %reshape.101 = bf16[4,2,7200]{2,1,0:T(2,128)(2,1)} reshape(bf16[128,15,30]{2,1,0:T(8,128)(2,1)S(1)} %copy.80) | data formatting | bytes 230400
  60.4 3.4 %all-to-all-start.3 = ((bf16[4,2,7200]{2,1,0:T(2,128)(2,1)}), bf16[4,2,7200]{2,1,0:T(2,128)(2,1)S(1)}, u32[]{:S(2)}, u32[]{:S(2)}) async-start(bf16[4,2,7200]{2,1,0:T(2,128)(2,1)} %reshape.101), calls=%async_computation.3 | async-start | bytes 233472 | tf_op jit(solution)/shard_map/all_to_all | solution.py:65
  63.8 16.8 %all_gather.12 = bf16[32,120,120]{2,0,1:T(8,128)(2,1)} all-gather(bf16[32,15,120]{2,0,1:T(8,128)(2,1)S(1)} %copy-done.3), channel_id=1, replica_groups=mesh['dap'=8,'ch'=4] {'dap'}, dimensions={1}, use_global_device_ids=true | all-gather | bytes 1036800 | tf_op jit(solution)/shard_map/all_gather | solution.py:66
  82.4 16.5 %all_gather.11 = bf16[32,120,120]{2,0,1:T(8,128)(2,1)S(1)} all-gather(bf16[32,15,120]{2,0,1:T(8,128)(2,1)S(1)} %all_to_all.72), channel_id=1, replica_groups=mesh['dap'=8,'ch'=4] {'dap'}, dimensions={1}, use_global_device_ids=true | all-gather | bytes 1036800 | tf_op jit(solution)/shard_map/all_gather | solution.py:68
  99.4 1.1 reshape.105
  100.5 4.2 %all-to-all-start.4 = ((bf16[4,2,7200]{2,1,0:T(2,128)(2,1)}), bf16[4,2,7200]{2,1,0:T(2,128)(2,1)S(1)}, u32[]{:S(2)}, u32[]{:S(2)}) async-start(bf16[4,2,7200]{2,1,0:T(2,128)(2,1)} %reshape.105), calls=%async_computation.4 | async-start | bytes 233472 | tf_op jit(solution)/shard_map/all_to_all | solution.py:77
  107.0 1.1 reshape.103
  108.1 1.5 %all-to-all-done.4 = bf16[4,2,7200]{2,1,0:T(2,128)(2,1)S(1)} async-done(((bf16[4,2,7200]{2,1,0:T(2,128)(2,1)}), bf16[4,2,7200]{2,1,0:T(2,128)(2,1)S(1)}, u32[]{:S(2)}, u32[]{:S(2)}) %all-to-all-start.4) | async-done | bytes 115232 | tf_op jit(solution)/shard_map/all_to_all | solution.py:77
  109.7 3.5 %all-to-all-start.5 = ((bf16[4,2,7200]{2,1,0:T(2,128)(2,1)}), bf16[4,2,7200]{2,1,0:T(2,128)(2,1)S(1)}, u32[]{:S(2)}, u32[]{:S(2)}) async-start(bf16[4,2,7200]{2,1,0:T(2,128)(2,1)} %reshape.103), calls=%async_computation.5 | async-start | bytes 233472 | tf_op jit(solution)/shard_map/all_to_all | solution.py:80
  114.5 1.5 %copy.86 = f32[4,32,15,30]{1,0,3,2:T(4,128)S(1)} copy(f32[4,32,15,30]{3,0,1,2:T(4,128)S(1)} %bitcast.67) | data formatting | bytes 460800 | tf_op jit(solution)/shard_map/convert_element_type | solution.py:84
  116.5 1.5 %all-to-all-done.5 = bf16[4,2,7200]{2,1,0:T(2,128)(2,1)S(1)} async-done(((bf16[4,2,7200]{2,1,0:T(2,128)(2,1)}), bf16[4,2,7200]{2,1,0:T(2,128)(2,1)S(1)}, u32[]{:S(2)}, u32[]{:S(2)}) %all-to-all-start.5) | async-done | bytes 115232 | tf_op jit(solution)/shard_map/all_to_all | solution.py:80
  119.3 1.5 %copy.91 = f32[4,32,15,30]{1,0,3,2:T(4,128)S(1)} copy(f32[4,32,15,30]{3,0,1,2:T(4,128)S(1)} %bitcast.68) | data formatting | bytes 460800 | tf_op jit(solution)/shard_map/convert_element_type | solution.py:85
  (83 shorter events, 21.9 us)
Async XLA Ops:
  0.6 2.2 %copy-start = (bf16[128,512]{1,0:T(8,128)(2,1)S(1)}, bf16[128,512]{1,0:T(8,128)(2,1)}, u32[]{:S(2)}) copy-start(bf16[128,512]{1,0:T(8,128)(2,1)} %param.8) | copy-start | bytes 393220
  0.6 1.1 copy-start.1
  2.0 0.7 copy-start.13
  5.2 10.2 %all-to-all-start.1 = ((bf16[4,2,7200]{2,1,0:T(2,128)(2,1)}), bf16[4,2,7200]{2,1,0:T(2,128)(2,1)S(1)}, u32[]{:S(2)}, u32[]{:S(2)}) async-start(bf16[4,2,7200]{2,1,0:T(2,128)(2,1)} %reshape.95), calls=%async_computation.1 | async-start | bytes 233472 | tf_op jit(solution)/shard_map/all_to_all | solution.py:45
  15.4 21.6 %all-to-all-start = ((bf16[4,2,7200]{2,1,0:T(2,128)(2,1)}), bf16[4,2,7200]{2,1,0:T(2,128)(2,1)S(1)}, u32[]{:S(2)}, u32[]{:S(2)}) async-start(bf16[4,2,7200]{2,1,0:T(2,128)(2,1)} %reshape.97), calls=%async_computation | async-start | bytes 233472 | tf_op jit(solution)/shard_map/all_to_all | solution.py:44
  38.2 0.6 copy-start.2
  55.1 0.8 copy-start.11
  55.8 0.8 copy-start.12
  56.6 1.0 copy-start.6
  56.6 1.0 copy-start.9
  57.6 0.7 copy-start.4
  60.4 3.5 %copy-start.3 = (bf16[32,15,120]{2,0,1:T(8,128)(2,1)S(1)}, bf16[32,15,120]{2,0,1:T(8,128)(2,1)}, u32[]{:S(2)}) copy-start(bf16[32,15,120]{2,0,1:T(8,128)(2,1)} %copy-done.2) | copy-start | bytes 345604
  60.4 20.2 %all-to-all-start.3 = ((bf16[4,2,7200]{2,1,0:T(2,128)(2,1)}), bf16[4,2,7200]{2,1,0:T(2,128)(2,1)S(1)}, u32[]{:S(2)}, u32[]{:S(2)}) async-start(bf16[4,2,7200]{2,1,0:T(2,128)(2,1)} %reshape.101), calls=%async_computation.3 | async-start | bytes 233472 | tf_op jit(solution)/shard_map/all_to_all | solution.py:65
  100.5 9.2 %all-to-all-start.4 = ((bf16[4,2,7200]{2,1,0:T(2,128)(2,1)}), bf16[4,2,7200]{2,1,0:T(2,128)(2,1)S(1)}, u32[]{:S(2)}, u32[]{:S(2)}) async-start(bf16[4,2,7200]{2,1,0:T(2,128)(2,1)} %reshape.105), calls=%async_computation.4 | async-start | bytes 233472 | tf_op jit(solution)/shard_map/all_to_all | solution.py:77
  104.7 1.2 copy-start.8
  109.7 8.3 %all-to-all-start.5 = ((bf16[4,2,7200]{2,1,0:T(2,128)(2,1)}), bf16[4,2,7200]{2,1,0:T(2,128)(2,1)S(1)}, u32[]{:S(2)}, u32[]{:S(2)}) async-start(bf16[4,2,7200]{2,1,0:T(2,128)(2,1)} %reshape.103), calls=%async_computation.5 | async-start | bytes 233472 | tf_op jit(solution)/shard_map/all_to_all | solution.py:80
  121.5 0.9 copy-start.5
  121.5 1.1 copy-start.7
  121.5 1.1 copy-start.10
where the time goes:
time: 125 us; the launch traced here: 124 us
  blocking collectives  59.2 us (47%)
  local copies, waits for them, and re-layouts  29.6 us (24%)
  starting transfers between devices  19.7 us (16%)
  waiting for transfers between devices  6.2 us (5%)
  matrix products  4.56 us (4%)
  other arithmetic  3.66 us (3%)
    all_gather x1, blocking collectives, on_device(): lax.all_gather(right_rows, 'dap', axis=1, tiled=True)  17 us
    all_gather x1, blocking collectives, on_device(): piece_left = lax.all_gather(left_rows, 'dap', axis=1, tiled=True)  16.8 us
    all_gather x1, blocking collectives, on_device(): piece_grad = lax.all_gather(grad_rows, 'dap', axis=1, tiled=True)  16.5 us
    unnamed x40, local copies, waits for them, and re-layouts  13.1 us
    all_to_all x1, blocking collectives, on_device(): lax.all_to_all(product, 'ch', split_axis=2, concat_axis=0, tiled=True)  8.94 us
    all_to_all x1, starting transfers between devices, on_device(): lax.all_to_all(right_cells, 'ch', split_axis=0, concat_axis=2, tiled=True)  5.19 us
    convert_element_type x3, local copies, waits for them, and re-layouts, on_device(): hidden_norm, hidden_scale = normalize(product_cells.astype(jnp.float32), 0)  4.68 us
    all_to_all x1, starting transfers between devices, on_device(): lax.all_to_all(new_left.astype(jnp.bfloat16), 'ch', split_axis=2, concat_...  4.21 us
  transfers between devices with their start and end apart: 5, of which 3 were waited for; matrix products, arithmetic and copies ran while one was open for 7% of the time, Pallas kernels for 0%

commit v1 on v0

--- a/solution.py
+++ b/solution.py
@@ -64,8 +64,11 @@
     grad_product = norm_back(grad_hidden, hidden_norm, hidden_scale, 0).astype(jnp.bfloat16)
     grad_rows = lax.all_to_all(grad_product, "ch", split_axis=0, concat_axis=2, tiled=True)
     piece_left = lax.all_gather(left_rows, "dap", axis=1, tiled=True)
-    piece_right = lax.all_gather(right_rows, "dap", axis=1, tiled=True)
-    piece_grad = lax.all_gather(grad_rows, "dap", axis=1, tiled=True)
+    piece_right, piece_grad = jnp.split(
+        lax.all_gather(jnp.concatenate([right_rows, grad_rows], axis=0), "dap", axis=1, tiled=True),
+        [right_rows.shape[0]],
+        axis=0,
+    )
     cross_slab = lax.dynamic_slice_in_dim(piece_grad, row_start, row_count, 2)
     new_left = jnp.einsum(
         "cij,cjk->cik", grad_rows, piece_right, preferred_element_type=jnp.float32

time: 125 us -> 140 us (1.12)
  between operations: 1.06 us -> 14.5 us
  waiting for transfers between devices: 6.2 us -> 15.2 us
  blocking collectives: 59.2 us -> 54.2 us
  starting transfers between devices: 19.7 us -> 15.4 us
  local copies, waits for them, and re-layouts: 29.6 us -> 25.9 us
  other arithmetic: 3.66 us -> 6.96 us
  matrix products: 4.56 us -> 7.02 us
    all_gather x1 -> x0, blocking collectives: 16.5 us -> none  [on_device(): piece_grad = lax.all_gather(grad_rows, 'dap', axis=1, tiled=True)]
    all_gather x0 -> x1, waiting for transfers between devices: none -> 9.69 us  [on_device(): lax.all_gather(jnp.concatenate([right_rows, grad_rows], axis=0), 'dap', a...]
    all_to_all x0 -> x1, blocking collectives: none -> 7.37 us  [on_device(): lax.all_to_all(grad_product, 'ch', split_axis=0, concat_axis=2, tiled=True)]
    all_gather x1, blocking collectives: 16.8 us -> 20.9 us  [on_device(): piece_left = lax.all_gather(left_rows, 'dap', axis=1, tiled=True)]
    all_to_all x1 -> x0, starting transfers between devices: 3.45 us -> none  [on_device(): lax.all_to_all(grad_product, 'ch', split_axis=0, concat_axis=2, tiled=True)]
    unnamed x40 -> x34, local copies, waits for them, and re-layouts: 13.1 us -> 9.88 us
    convert_element_type x3, local copies, waits for them, and re-layouts: 4.68 us -> 2.36 us  [on_device(): hidden_norm, hidden_scale = normalize(product_cells.astype(jnp.float32), 0)]
    split x0 -> x1, local copies, waits for them, and re-layouts: none -> 1.86 us  [on_device(): jnp.split(lax.all_gather(jnp.concatenate([right_rows, grad_rows], axis=0)...]
  transfers between devices with their start and end apart: 5 -> 5, of which waited for: 3 -> 4; matrix products, arithmetic and copies ran while one was open for 7% -> 7% of each run, Pallas kernels for 0% -> 0%
where the time goes in v1:
time: 140 us; the launch traced here: 139 us
  blocking collectives  54.2 us (39%)
  local copies, waits for them, and re-layouts  25.9 us (18%)
  starting transfers between devices  15.4 us (11%)
  waiting for transfers between devices  15.2 us (11%)
  between operations  14.5 us (10%)
  matrix products  7.02 us (5%)
  other arithmetic  6.96 us (5%)
    all_gather x1, blocking collectives, on_device(): piece_left = lax.all_gather(left_rows, 'dap', axis=1, tiled=True)  20.9 us
    all_gather x1, blocking collectives, on_device(): lax.all_gather(right_rows, 'dap', axis=1, tiled=True)  17 us
    unnamed x34, local copies, waits for them, and re-layouts  9.88 us
    all_gather x1, waiting for transfers between devices, on_device(): lax.all_gather(jnp.concatenate([right_rows, grad_rows], axis=0), 'dap', a...  9.69 us
    all_to_all x1, blocking collectives, on_device(): lax.all_to_all(product, 'ch', split_axis=2, concat_axis=0, tiled=True)  8.89 us
    all_to_all x1, blocking collectives, on_device(): lax.all_to_all(grad_product, 'ch', split_axis=0, concat_axis=2, tiled=True)  7.37 us
    all_to_all x1, starting transfers between devices, on_device(): lax.all_to_all(right_cells, 'ch', split_axis=0, concat_axis=2, tiled=True)  5.19 us
    all_to_all x1, starting transfers between devices, on_device(): lax.all_to_all(new_right.astype(jnp.bfloat16), 'ch', split_axis=2, concat...  3.54 us
  transfers between devices with their start and end apart: 5, of which 4 were waited for; matrix products, arithmetic and copies ran while one was open for 7% of the time, Pallas kernels for 0%

profile of v1, /device:TPU:0, one launch (start us, length us, event | category | flops | bytes accessed | tf_op | source)
XLA Modules:
  0.0 139.2 jit_solution(12418385377730111434)
XLA Ops:
  8.3 1.2 fusion.24
  10.3 1.2 convolution_bitcast_fusion
  12.2 1.3 reshape.95
  13.5 5.2 %all-to-all-start.1 = ((bf16[4,2,7200]{2,1,0:T(2,128)(2,1)}), bf16[4,2,7200]{2,1,0:T(2,128)(2,1)S(1)}, u32[]{:S(2)}, u32[]{:S(2)}) async-start(bf16[4,2,7200]{2,1,0:T(2,128)(2,1)} %reshape.95), calls=%async_computation.1 | async-start | bytes 233472 | tf_op jit(solution)/shard_map/all_to_all | solution.py:45
  19.2 1.3 reshape.97
  20.5 3.2 %all-to-all-done.1 = bf16[4,2,7200]{2,1,0:T(2,128)(2,1)S(1)} async-done(((bf16[4,2,7200]{2,1,0:T(2,128)(2,1)}), bf16[4,2,7200]{2,1,0:T(2,128)(2,1)S(1)}, u32[]{:S(2)}, u32[]{:S(2)}) %all-to-all-start.1) | async-done | bytes 115232 | tf_op jit(solution)/shard_map/all_to_all | solution.py:45
  23.7 3.3 %all-to-all-start = ((bf16[4,2,7200]{2,1,0:T(2,128)(2,1)}), bf16[4,2,7200]{2,1,0:T(2,128)(2,1)S(1)}, u32[]{:S(2)}, u32[]{:S(2)}) async-start(bf16[4,2,7200]{2,1,0:T(2,128)(2,1)} %reshape.97), calls=%async_computation | async-start | bytes 233472 | tf_op jit(solution)/shard_map/all_to_all | solution.py:44
  28.3 17.0 %all_gather.9 = bf16[32,120,120]{2,0,1:T(8,128)(2,1)S(1)} all-gather(bf16[32,15,120]{2,0,1:T(8,128)(2,1)S(1)} %all_to_all.67), channel_id=1, replica_groups=mesh['dap'=8,'ch'=4] {'dap'}, dimensions={1}, use_global_device_ids=true | all-gather | bytes 1036800 | tf_op jit(solution)/shard_map/all_gather | solution.py:50
  48.1 8.9 %all_to_all.81 = bf16[4,2,7200]{2,1,0:T(2,128)(2,1)S(1)} all-to-all(bf16[4,2,7200]{2,1,0:T(2,128)(2,1)S(1)} %reshape.99), channel_id=1, replica_groups=mesh['dap'=8,'ch'=4] {'ch'}, dimensions={0} | all-to-all | bytes 230400 | tf_op jit(solution)/shard_map/all_to_all | solution.py:53
  58.5 1.5 %copy.81 = f32[4,32,15,30]{1,0,3,2:T(4,128)S(1)} copy(f32[4,32,15,30]{3,0,1,2:T(4,128)S(1)} %bitcast.66) | data formatting | bytes 460800 | tf_op jit(solution)/shard_map/convert_element_type | solution.py:54
  61.9 1.8 %multiply_convert_fusion.5 = (bf16[15,30,128]{2,1,0:T(8,128)(2,1)}, f32[15,30,128]{2,1,0:T(8,128)S(1)}) fusion(f32[15,30,128]{2,1,0:T(8,128)S(1)} %fusion.40, bf16[128,128]{1,0:T(8,128)(2,1)} %param.9, bf16[15,30,128]{2,1,0:T(8,128)(2,1)S(1)} %copy-done.1, f32[15,30]{1,0:T(8,128)S(1)} %add_rsqrt_fusion.1, f32[15,30]{1,0:T(8,128)S(1)} %broadcast_multiply_fusion.6), kind=kOutput, calls=%fused_computation.59 | convolution fusion | flops 15264000 | bytes 727568 | tf_op jit(solution)/shard_map/rkd,de->rke/dot_general | solution.py:41
  65.6 7.4 %all_to_all.82 = bf16[4,2,7200]{2,1,0:T(2,128)(2,1)S(1)} all-to-all(bf16[4,2,7200]{2,1,0:T(2,128)(2,1)S(1)} %reshape.101), channel_id=1, replica_groups=mesh['dap'=8,'ch'=4] {'ch'}, dimensions={0} | all-to-all | bytes 230400 | tf_op jit(solution)/shard_map/all_to_all | solution.py:65
  75.0 20.9 %all_gather.11 = bf16[32,120,120]{2,0,1:T(8,128)(2,1)} all-gather(bf16[32,15,120]{2,0,1:T(8,128)(2,1)S(1)} %all_to_all.63), channel_id=1, replica_groups=mesh['dap'=8,'ch'=4] {'dap'}, dimensions={1}, use_global_device_ids=true | all-gather | bytes 1036800 | tf_op jit(solution)/shard_map/all_gather | solution.py:66
  95.8 9.7 %all-gather.2.cloned.1.call-done = bf16[64,120,120]{2,0,1:T(8,128)(2,1)} async-done(((bf16[64,15,120]{2,0,1:T(8,128)(2,1)}), bf16[64,120,120]{2,0,1:T(8,128)(2,1)}) %all-gather.2.cloned.1.call-update) | async-done | bytes 1843216 | tf_op jit(solution)/shard_map/all_gather | solution.py:68
  105.5 1.9 %fusion.57 = (bf16[32,120,120]{2,0,1:T(8,128)(2,1)S(1)}, bf16[32,120,120]{2,0,1:T(8,128)(2,1)S(1)}) fusion(bf16[64,120,120]{2,0,1:T(8,128)(2,1)} %all-gather.2.cloned.1.call-done), kind=kLoop, calls=%fused_computation.91 | loop fusion | bytes 3686400 | tf_op jit(solution)/shard_map/split | solution.py:67
  108.4 1.1 reshape.105
  109.5 3.3 %all-to-all-start.4 = ((bf16[4,2,7200]{2,1,0:T(2,128)(2,1)}), bf16[4,2,7200]{2,1,0:T(2,128)(2,1)S(1)}, u32[]{:S(2)}, u32[]{:S(2)}) async-start(bf16[4,2,7200]{2,1,0:T(2,128)(2,1)} %reshape.105), calls=%async_computation.4 | async-start | bytes 233472 | tf_op jit(solution)/shard_map/all_to_all | solution.py:80
  115.2 1.1 reshape.103
  116.3 1.5 %all-to-all-done.4 = bf16[4,2,7200]{2,1,0:T(2,128)(2,1)S(1)} async-done(((bf16[4,2,7200]{2,1,0:T(2,128)(2,1)}), bf16[4,2,7200]{2,1,0:T(2,128)(2,1)S(1)}, u32[]{:S(2)}, u32[]{:S(2)}) %all-to-all-start.4) | async-done | bytes 115232 | tf_op jit(solution)/shard_map/all_to_all | solution.py:80
  117.8 3.5 %all-to-all-start.5 = ((bf16[4,2,7200]{2,1,0:T(2,128)(2,1)}), bf16[4,2,7200]{2,1,0:T(2,128)(2,1)S(1)}, u32[]{:S(2)}, u32[]{:S(2)}) async-start(bf16[4,2,7200]{2,1,0:T(2,128)(2,1)} %reshape.103), calls=%async_computation.5 | async-start | bytes 233472 | tf_op jit(solution)/shard_map/all_to_all | solution.py:83
  122.7 1.5 %copy.88 = f32[4,32,15,30]{1,0,3,2:T(4,128)S(1)} copy(f32[4,32,15,30]{3,0,1,2:T(4,128)S(1)} %bitcast.67) | data formatting | bytes 460800 | tf_op jit(solution)/shard_map/convert_element_type | solution.py:87
  124.1 1.1 reshape.86
  127.4 1.5 %copy.93 = f32[4,32,15,30]{1,0,3,2:T(4,128)S(1)} copy(f32[4,32,15,30]{3,0,1,2:T(4,128)S(1)} %bitcast.68) | data formatting | bytes 460800 | tf_op jit(solution)/shard_map/convert_element_type | solution.py:88
  129.3 1.3 multiply_convert_fusion.3
  (80 shorter events, 23.1 us)
Async XLA Ops:
  7.2 3.1 %copy-start = (bf16[128,512]{1,0:T(8,128)(2,1)S(1)}, bf16[128,512]{1,0:T(8,128)(2,1)}, u32[]{:S(2)}) copy-start(bf16[128,512]{1,0:T(8,128)(2,1)} %param.8) | copy-start | bytes 393220
  13.5 10.2 %all-to-all-start.1 = ((bf16[4,2,7200]{2,1,0:T(2,128)(2,1)}), bf16[4,2,7200]{2,1,0:T(2,128)(2,1)S(1)}, u32[]{:S(2)}, u32[]{:S(2)}) async-start(bf16[4,2,7200]{2,1,0:T(2,128)(2,1)} %reshape.95), calls=%async_computation.1 | async-start | bytes 233472 | tf_op jit(solution)/shard_map/all_to_all | solution.py:45
  23.7 21.6 %all-to-all-start = ((bf16[4,2,7200]{2,1,0:T(2,128)(2,1)}), bf16[4,2,7200]{2,1,0:T(2,128)(2,1)S(1)}, u32[]{:S(2)}, u32[]{:S(2)}) async-start(bf16[4,2,7200]{2,1,0:T(2,128)(2,1)} %reshape.97), calls=%async_computation | async-start | bytes 233472 | tf_op jit(solution)/shard_map/all_to_all | solution.py:44
  27.0 78.5 %all-gather.2.cloned.1.call-start = ((), (), s32[]{:S(2)}) async-start(), calls=%async_computation.6 | async-start | bytes 2211840 | tf_op jit(solution)/shard_map/all_gather | solution.py:68
  28.3 18.9 %copy-start.2 = (bf16[32,15,120]{2,0,1:T(8,128)(2,1)}, bf16[32,15,120]{2,0,1:T(8,128)(2,1)S(1)}, u32[]{:S(2)}) copy-start(bf16[32,15,120]{2,0,1:T(8,128)(2,1)S(1)} %all_to_all.67) | copy-start | bytes 345604
  58.5 3.4 %copy-start.1 = (bf16[15,30,128]{2,1,0:T(8,128)(2,1)S(1)}, bf16[15,30,128]{2,1,0:T(8,128)(2,1)}, u32[]{:S(2)}) copy-start(bf16[15,30,128]{2,1,0:T(8,128)(2,1)} %param.6) | copy-start | bytes 345604
  60.4 3.2 %copy-start.7 = (bf16[15,30,128]{2,1,0:T(8,128)(2,1)S(1)}, bf16[15,30,128]{2,1,0:T(8,128)(2,1)}, u32[]{:S(2)}) copy-start(bf16[15,30,128]{2,1,0:T(8,128)(2,1)} %param.11) | copy-start | bytes 345604
  60.4 3.2 %copy-start.9 = (bf16[128,128]{1,0:T(8,128)(2,1)S(1)}, bf16[128,128]{1,0:T(8,128)(2,1)}, u32[]{:S(2)}) copy-start(bf16[128,128]{1,0:T(8,128)(2,1)} %param.10) | copy-start | bytes 98308
  61.9 2.2 %copy-start.4 = (f32[15,30,128]{2,1,0:T(8,128)}, f32[15,30,128]{2,1,0:T(8,128)S(1)}, u32[]{:S(2)}) copy-start(f32[15,30,128]{2,1,0:T(8,128)S(1)} %fusion.40) | copy-start | bytes 691204
  64.4 9.7 %copy-start.3 = (bf16[32,15,120]{2,0,1:T(8,128)(2,1)S(1)}, bf16[32,15,120]{2,0,1:T(8,128)(2,1)}, u32[]{:S(2)}) copy-start(bf16[32,15,120]{2,0,1:T(8,128)(2,1)} %copy-done.2) | copy-start | bytes 345604
  109.5 8.3 %all-to-all-start.4 = ((bf16[4,2,7200]{2,1,0:T(2,128)(2,1)}), bf16[4,2,7200]{2,1,0:T(2,128)(2,1)S(1)}, u32[]{:S(2)}, u32[]{:S(2)}) async-start(bf16[4,2,7200]{2,1,0:T(2,128)(2,1)} %reshape.105), calls=%async_computation.4 | async-start | bytes 233472 | tf_op jit(solution)/shard_map/all_to_all | solution.py:80
  112.8 1.2 copy-start.6
  117.8 8.3 %all-to-all-start.5 = ((bf16[4,2,7200]{2,1,0:T(2,128)(2,1)}), bf16[4,2,7200]{2,1,0:T(2,128)(2,1)S(1)}, u32[]{:S(2)}, u32[]{:S(2)}) async-start(bf16[4,2,7200]{2,1,0:T(2,128)(2,1)} %reshape.103), calls=%async_computation.5 | async-start | bytes 233472 | tf_op jit(solution)/shard_map/all_to_all | solution.py:83
  129.3 1.6 %copy-start.5 = (f32[15,30,128]{2,1,0:T(8,128)S(1)}, f32[15,30,128]{2,1,0:T(8,128)}, u32[]{:S(2)}) copy-start(f32[15,30,128]{2,1,0:T(8,128)} %copy-done.4) | copy-start | bytes 691204
  129.3 1.6 %copy-start.8 = (bf16[15,30,128]{2,1,0:T(8,128)(2,1)S(1)}, bf16[15,30,128]{2,1,0:T(8,128)(2,1)}, u32[]{:S(2)}) copy-start(bf16[15,30,128]{2,1,0:T(8,128)(2,1)} %param.11) | copy-start | bytes 345604
  129.3 1.6 %copy-start.10 = (bf16[128,128]{1,0:T(8,128)(2,1)S(1)}, bf16[128,128]{1,0:T(8,128)(2,1)}, u32[]{:S(2)}) copy-start(bf16[128,128]{1,0:T(8,128)(2,1)} %param.9) | copy-start | bytes 98308
Sparse Core Ops, SparseCore 0:
  75.1 30.4 all-gather.1
